TPU v7x, 256 devices: a whole 4x4x8 slice. The times are simulated.
256 devices in a mesh: context: 64 (over z, x, core), head: 4 (over y).
Axes of the slice: x: 4, y: 4, z: 8, core: 2. Of those that a mesh axis runs over, the one named last changes fastest.
Arguments:
- queries: bfloat16 [32768, 4096], P(('context', 'head')), may hold values from -6 to 6
- key_input: bfloat16 [32768, 4096], P(('context', 'head')), may hold values from -32 to 32
- value_input: bfloat16 [32768, 4096], P(('context', 'head')), may hold values from -32 to 32
- gate_input: bfloat16 [32768, 4096], P(('context', 'head')), may hold values from -6 to 6
- decay_logit: float32 [32768, 32], P(('context', 'head')), may hold values from -5 to 16
- beta_logit: float32 [32768, 32], P(('context', 'head')), may hold values from -9 to 9
- decay_bias: float32 [32], P('head'), may hold values from -16 to -3
- norm_gain: float32 [128], replicated, may hold values from 0.1 to 1.9
- doc_start: int32 [512], P('context'), may hold values from 0 to 1, as said below
Outputs:
- layer_output: bfloat16 [32768, 4096], P(('context', 'head'))
Inputs may be any that keep to these rules, and one draw needn't show every extreme that they name: `doc_start`: exactly one of the groups 1 to max(3, 64) holds a 1; apart from it, 1 appears only in the last max(2, 64) groups.
All inputs are finite; a program needn't handle non-finite values.
Results may differ from a plain program's by a relative error of at most 0.013.
Values may be sent and summed in bfloat16 or wider, within the bound.
A program may use at most 192 MiB of HBM per device.

v0:
```python
import jax
import jax.numpy as jnp
from jax import lax
from jax.sharding import PartitionSpec as P

C = 64


PRECISE = lax.Precision.HIGHEST


def carried_in(shard, axis, join, neutral):
    place = lax.axis_index(axis)
    gathered = jax.tree.map(
        lambda a, kind: lax.all_gather(a.astype(kind), axis),
        shard,
        jax.tree.map(lambda a: jnp.bfloat16 if a.dtype == jnp.float32 else a.dtype, shard),
    )
    state = jax.tree.map(lambda a, e: jnp.zeros_like(a) + jnp.asarray(e, a.dtype), shard, neutral)

    def one(hop, state):
        return join(
            state,
            jax.tree.map(
                lambda a, own: lax.dynamic_index_in_dim(a, hop, 0, False).astype(own.dtype),
                gathered,
                shard,
            ),
        )

    return lax.fori_loop(0, place, one, state)


def gated_norm(core_rows, gate_input, norm_gain):
    row_count = core_rows.shape[0]
    widened = core_rows.astype(jnp.float32).reshape(row_count, -1, norm_gain.shape[0])
    scaled = widened * lax.rsqrt(jnp.mean(widened * widened, axis=-1, keepdims=True) + 1e-06)
    gate_wide = gate_input.astype(jnp.float32).reshape(widened.shape)
    result = scaled * norm_gain * jax.nn.silu(gate_wide)
    return result.reshape(row_count, -1).astype(jnp.bfloat16)


def carried_part(query_blocks, gammas, query_mix, solved_keys, entering):
    through = (
        jnp.einsum("nthd,nhde->nthe", query_blocks, entering, precision=PRECISE)
        * gammas[:, :, :, None]
    )
    key_state = jnp.einsum("nhsd,nhde->nhse", solved_keys, entering, precision=PRECISE)
    return through - jnp.einsum("nhts,nhse->nthe", query_mix, key_state, precision=PRECISE)


def compose(earlier, later):
    product = jnp.einsum("hde,hef->hdf", later[0], earlier[0], precision=PRECISE)
    summed = jnp.einsum("hde,hef->hdf", later[0], earlier[1], precision=PRECISE) + later[1]
    return (product, summed)


def body(
    queries,
    key_input,
    value_input,
    gate_input,
    decay_logit,
    beta_logit,
    decay_bias,
    norm_gain,
    doc_start,
):
    query_rows, key_rows, value_rows = (
        lax.all_to_all(queries, "head", split_axis=1, concat_axis=0, tiled=True),
        lax.all_to_all(key_input, "head", split_axis=1, concat_axis=0, tiled=True),
        lax.all_to_all(value_input, "head", split_axis=1, concat_axis=0, tiled=True),
    )
    decay_rows, beta_rows = (
        lax.all_to_all(
            decay_logit.astype(jnp.bfloat16), "head", split_axis=1, concat_axis=0, tiled=True
        ).astype(decay_logit.dtype),
        lax.all_to_all(
            beta_logit.astype(jnp.bfloat16), "head", split_axis=1, concat_axis=0, tiled=True
        ).astype(beta_logit.dtype),
    )
    length = decay_rows.shape[0]
    head_count = decay_rows.shape[1]
    groups = length // C
    key_width = key_rows.shape[1] // head_count
    value_width = value_rows.shape[1] // head_count
    log_decay = -jax.nn.softplus(decay_rows + decay_bias[None, :])
    beta_gate = jax.nn.sigmoid(beta_rows)
    query_blocks = query_rows.reshape(groups, C, head_count, key_width)
    raw_keys = key_rows.reshape(groups, C, head_count, key_width).astype(jnp.float32)
    normed = (
        raw_keys * lax.rsqrt(jnp.sum(raw_keys * raw_keys, axis=-1, keepdims=True) + 1e-06)
    ).astype(jnp.bfloat16)
    value_blocks = value_rows.reshape(groups, C, head_count, value_width)
    cum_decay = jnp.cumsum(log_decay.reshape(groups, C, head_count), axis=1)
    beta_blocks = beta_gate.reshape(groups, C, head_count)
    row_index = lax.broadcasted_iota(jnp.int32, (C, C), 0)
    column_index = lax.broadcasted_iota(jnp.int32, (C, C), 1)
    cum_heads = jnp.transpose(cum_decay, (0, 2, 1))
    decay_gap = cum_heads[:, :, :, None] - cum_heads[:, :, None, :]
    strict = jnp.exp(jnp.where(row_index > column_index, decay_gap, -jnp.inf))
    inclusive = jnp.exp(jnp.where(row_index >= column_index, decay_gap, -jnp.inf))
    key_gram = jnp.einsum("nthd,nshd->nhts", normed, normed, preferred_element_type=jnp.float32)
    query_gram = jnp.einsum(
        "nthd,nshd->nhts", query_blocks, normed, preferred_element_type=jnp.float32
    )
    lower_part = jnp.transpose(beta_blocks, (0, 2, 1))[:, :, :, None] * strict * key_gram
    scaled_keys = (beta_blocks * jnp.exp(cum_decay))[:, :, :, None] * normed
    scaled_values = beta_blocks[:, :, :, None] * value_blocks
    right_side = jnp.transpose(jnp.concatenate([scaled_keys, scaled_values], axis=-1), (0, 2, 1, 3))
    solved = jax.scipy.linalg.solve_triangular(
        jnp.eye(C, dtype=jnp.float32) + lower_part, right_side, lower=True, unit_diagonal=True
    )
    solved_keys = solved[:, :, :, :key_width]
    solved_values = solved[:, :, :, key_width:]
    query_mix = inclusive * query_gram
    gammas = jnp.exp(cum_decay)
    last_cum = cum_decay[:, -1, :]
    back_keys = jnp.exp(last_cum[:, None, :] - cum_decay)[:, :, :, None] * normed
    keep_mask = 1.0 - doc_start.astype(jnp.float32)
    identity = jnp.eye(key_width, dtype=jnp.float32)
    transition = keep_mask[:, None, None, None] * (
        jnp.exp(last_cum)[:, :, None, None] * identity
        - jnp.einsum("nthd,nhte->nhde", back_keys, solved_keys, precision=PRECISE)
    )
    update = jnp.einsum("nthd,nhte->nhde", back_keys, solved_values, precision=PRECISE)
    eye_state = jnp.broadcast_to(identity, (head_count, key_width, key_width))
    zero_state = jnp.zeros((head_count, key_width, value_width), jnp.float32)

    def extend(carry, group_terms):
        step_matrix, step_update = group_terms
        product = jnp.einsum("hde,hef->hdf", step_matrix, carry[0], precision=PRECISE)
        summed = jnp.einsum("hde,hef->hdf", step_matrix, carry[1], precision=PRECISE) + step_update
        return ((product, summed), carry)

    totals = lax.scan(extend, (eye_state, zero_state), (transition, update))[0]
    carried = carried_in(totals, "context", compose, (eye_state, zero_state))[1]

    def replay(state_in, group_terms):
        (
            step_matrix,
            step_update,
            query_group,
            gamma_group,
            mix_group,
            keys_group,
            values_group,
            keep_group,
        ) = group_terms
        entering = (keep_group * state_in)[None]
        local_part = jnp.einsum("hts,hse->the", mix_group, values_group, precision=PRECISE)
        out_group = (
            local_part
            + carried_part(
                query_group[None], gamma_group[None], mix_group[None], keys_group[None], entering
            )[0]
        )
        new_state = (
            jnp.einsum("hde,hef->hdf", step_matrix, state_in, precision=PRECISE) + step_update
        )
        return (new_state, out_group)

    core_blocks = lax.scan(
        replay,
        carried,
        (
            transition,
            update,
            query_blocks,
            gammas,
            query_mix,
            solved_keys,
            solved_values,
            keep_mask,
        ),
    )[1]
    core_rows = core_blocks.reshape(length, head_count * value_width).astype(jnp.bfloat16)
    returned = lax.all_to_all(core_rows, "head", split_axis=0, concat_axis=1, tiled=True)
    return gated_norm(returned, gate_input, norm_gain)


def solution(mesh):
    return jax.shard_map(
        body,
        mesh=mesh,
        in_specs=(
            P(("context", "head"), None),
            P(("context", "head"), None),
            P(("context", "head"), None),
            P(("context", "head"), None),
            P(("context", "head"), None),
            P(("context", "head"), None),
            P("head"),
            P(),
            P("context"),
        ),
        out_specs=P(("context", "head"), None),
        check_vma=False,
    )
```

profile of v0, /device:TPU:231, one launch (start us, length us, event | category | flops | bytes accessed | tf_op | source)
XLA Modules:
  0.0 837.6 jit_solution(14945289725504027375)
XLA Ops:
  7.9 4.2 all-to-all-start
  14.2 2.3 copy.137
  17.6 4.2 all-to-all-start.2
  22.2 6.3 fusion.79
  28.6 4.2 all-to-all-start.1
  33.6 12.3 %all-to-all-done.1 = bf16[128,4,1024]{2,0,1:T(8,128)(2,1)S(1)} async-done(((bf16[128,4,1024]{2,0,1:T(8,128)(2,1)}), bf16[128,4,1024]{2,0,1:T(8,128)(2,1)S(1)}, u32[]{:S(2)}, u32[]{:S(2)}) %all-to-all-start.1) | async-done | bytes 1048608 | tf_op jit(solution)/shard_map/all_to_all | solution.py:71
  45.9 4.3 all-to-all-start.3
  51.8 2.4 convert_multiply_fusion.2
  56.3 315.3 %custom-call.4 = f32[8,8,1,64,64]{3,4,2,1,0:T(8,128)} custom-call(f32[8,8,1,64,64]{4,3,2,1,0:T(8,128)S(1)} %fusion.58), custom_call_target="InvertDiagBlocksLowerTriangular" | custom-call | tf_op jit(solution)/shard_map/jit(_solve_triangular)/vmap(vmap())/triangular_solve | solution.py:111
  375.8 4.2 fusion.42
  380.0 8.9 %fusion.45 = f32[8,8,128,128]{3,2,1,0:T(8,128)} fusion(bf16[8,64,8,128]{3,1,2,0:T(8,128)(2,1)S(1)} %copy-done.4, f32[8,64,8]{1,2,0:T(8,128)S(1)} %copy.93, f32[8,8,64,256]{3,2,1,0:T(8,128)S(1)} %fusion.42), kind=kOutput, calls=%fused_computation.62 | convolution fusion | flops 806354944 | bytes 7372800 | tf_op jit(solution)/shard_map/nthd,nhte->nhde/dot_general | solution.py:126
  389.0 9.5 %subtract_multiply_fusion = f32[8,8,128,128]{3,2,1,0:T(8,128)} fusion(bf16[8,64,8,128]{3,1,2,0:T(8,128)(2,1)S(1)} %copy-done.4, f32[128,128]{1,0:T(8,128)S(1)} %fusion.67, f32[8,8]{1,0:T(8,128)S(1)} %fusion.72, f32[8]{0:T(128)S(1)} %convert_subtract_fusion, f32[8,64,8]{1,2,0:T(8,128)S(1)} %copy.93, f32[8,8,64,256]{3,2,1,0:T(8,128)S(1)} %fusion.42), kind=kOutput, calls=%fused_computation.53 | convolution fusion | flops 809500672 | bytes 7442944 | tf_op jit(solution)/shard_map/nthd,nhte->nhde/dot_general | solution.py:124
  398.5 29.6 %while.39 = (s32[]{:T(128)}, f32[8,128,128]{2,1,0:T(8,128)S(1)}, f32[8,128,128]{2,1,0:T(8,128)S(1)}, f32[8,8,128,128]{3,2,1,0:T(8,128)}, f32[8,8,128,128]{3,2,1,0:T(8,128)}, /*index=5*/s32[]{:T(128)}, s32[]{:T(128)}) while((s32[]{:T(128)}, f32[8,128,128]{2,1,0:T(8,128)S(1)}, f32[8,128,128]{2,1,0:T(8,128)S(1)}, ...), condition=%wide.region_3.4_spmd.clone, body=%wide.region_2.3_spmd.clone.sunk | while | flops 402915328 | bytes 5768791 | solution.py:136
  429.8 2.3 copy.135
  432.1 4.1 all-to-all-start.4
  436.4 11.3 %all-to-all-done.4 = bf16[128,4,1024]{2,0,1:T(8,128)(2,1)S(1)} async-done(((bf16[128,4,1024]{2,0,1:T(8,128)(2,1)}), bf16[128,4,1024]{2,0,1:T(8,128)(2,1)S(1)}, u32[]{:S(2)}, u32[]{:S(2)}) %all-to-all-start.4) | async-done | bytes 1048608 | tf_op jit(solution)/shard_map/all_to_all | solution.py:70
  454.1 73.7 %all-gather.5.cloned.1.call-done = bf16[512,128,128]{2,1,0:T(8,128)(2,1)} async-done(((bf16[8,128,128]{2,1,0:T(8,128)(2,1)}), bf16[512,128,128]{2,1,0:T(8,128)(2,1)}) %all-gather.5.cloned.1.call-update) | async-done | bytes 16777232 | tf_op jit(solution)/shard_map/all_gather | solution.py:15
  527.8 99.0 %all-gather.7.cloned.1.call-done = bf16[512,128,128]{2,1,0:T(8,128)(2,1)} async-done(((bf16[8,128,128]{2,1,0:T(8,128)(2,1)}), bf16[512,128,128]{2,1,0:T(8,128)(2,1)}) %all-gather.7.cloned.1.call-update) | async-done | bytes 16777232 | tf_op jit(solution)/shard_map/all_gather | solution.py:15
  626.9 96.0 %while.37 = (s32[]{:T(128)}, f32[8,128,128]{2,1,0:T(8,128)S(1)}, s32[]{:T(128)}, bf16[64,8,128,128]{3,2,1,0:T(8,128)(2,1)}, bf16[64,8,128,128]{3,2,1,0:T(8,128)(2,1)}, /*index=5*/s32[]{:T(128)}, s32[]{:T(128)}, s32[]{:T(128)}) while((s32[]{:T(128)}, f32[8,128,128]{2,1,0:T(8,128)S(1)}, s32[]{:T(128)}, bf16[64,8,128,128]{3,2,1,0:T(8,128)(2,1)}, ...), condition=%wide.region_5.6_spmd, body=%wide.region_4.5_spmd.sunk | while | flops 201588736 | bytes 2622583 | solution.py:31
  722.9 74.4 %while.38 = (s32[]{:T(128)}, f32[8,128,128]{2,1,0:T(8,128)S(1)}, bf16[8,64,8,128]{3,1,2,0:T(8,128)(2,1)}, f32[8,8,128,128]{3,2,1,0:T(8,128)}, f32[8,8,128,128]{3...) while((s32[]{:T(128)}, f32[8,128,128]{2,1,0:T(8,128)S(1)}, ...), condition=%wide.region_7.8_spmd, body=%wide.region_6.7_spmd.sunk | while | flops 503906304 | bytes 7219341 | solution.py:163
  746.8 2.1 fusion.122
  800.5 4.0 all-to-all-start.5
  805.8 13.5 %all-to-all-done.5 = bf16[4,128,1024]{2,1,0:T(8,128)(2,1)S(1)} async-done(((bf16[4,128,1024]{2,1,0:T(8,128)(2,1)}), bf16[4,128,1024]{2,1,0:T(8,128)(2,1)S(1)}, u32[]{:S(2)}, u32[]{:S(2)}) %all-to-all-start.5) | async-done | bytes 1048608 | tf_op jit(solution)/shard_map/all_to_all | solution.py:178
  828.5 2.3 copy.116
  (307 shorter events, 229.9 us)
Async XLA Ops:
  6.5 799.3 %copy-start = (f32[128]{0:T(128)S(1)}, f32[128]{0:T(128)}, u32[]{:S(2)}) copy-start(f32[128]{0:T(128)} %param.22) | copy-start | bytes 1540
  6.5 10.0 %copy-start.8 = (bf16[128,4096]{1,0:T(8,128)(2,1)S(1)}, bf16[128,4096]{1,0:T(8,128)(2,1)}, u32[]{:S(2)}) copy-start(bf16[128,4096]{1,0:T(8,128)(2,1)} %param.17) | copy-start | bytes 3145732
  7.9 9.7 %all-to-all-start = ((bf16[128,4,8]{0,2,1:T(8,128)(2,1)}), bf16[128,4,8]{0,2,1:T(8,128)(2,1)S(1)}, u32[]{:S(2)}, u32[]{:S(2)}) async-start(bf16[128,4,8]{0,2,1:T(8,128)(2,1)} %convert_bitcast_fusion.3), calls=%async_computation | async-start | bytes 16384 | tf_op jit(solution)/shard_map/all_to_all | solution.py:75
  14.2 7.7 copy-start.10
  17.6 10.9 %all-to-all-start.2 = ((bf16[128,4,8]{0,2,1:T(8,128)(2,1)}), bf16[128,4,8]{0,2,1:T(8,128)(2,1)S(1)}, u32[]{:S(2)}, u32[]{:S(2)}) async-start(bf16[128,4,8]{0,2,1:T(8,128)(2,1)} %convert_bitcast_fusion.2), calls=%async_computation.2 | async-start | bytes 16384 | tf_op jit(solution)/shard_map/all_to_all | solution.py:78
  28.6 17.4 %all-to-all-start.1 = ((bf16[128,4,1024]{2,0,1:T(8,128)(2,1)}), bf16[128,4,1024]{2,0,1:T(8,128)(2,1)S(1)}, u32[]{:S(2)}, u32[]{:S(2)}) async-start(bf16[128,4,1024]{2,0,1:T(8,128)(2,1)} %bitcast.149), calls=%async_computation.1 | async-start | bytes 2097152 | tf_op jit(solution)/shard_map/all_to_all | solution.py:71
  45.9 325.7 %all-to-all-start.3 = ((bf16[128,4,1024]{2,0,1:T(8,128)(2,1)}), bf16[128,4,1024]{2,0,1:T(8,128)(2,1)}, u32[]{:S(2)}, u32[]{:S(2)}) async-start(bf16[128,4,1024]{2,0,1:T(8,128)(2,1)} %bitcast.148), calls=%async_computation.3 | async-start | bytes 2097152 | tf_op jit(solution)/shard_map/all_to_all | solution.py:72
  50.2 477.6 %all-gather.5.cloned.1.call-start = ((), (), s32[]{:S(2)}) async-start(), calls=%async_computation.6 | async-start | bytes 17039360 | tf_op jit(solution)/shard_map/all_gather | solution.py:15
  54.1 1.0 copy-start.3
  373.6 1.6 copy-start.5
  373.6 2.2 copy-start.7
  375.8 4.2 copy-start.4
  380.0 9.0 %copy-start.1 = (f32[8,8,64,256]{3,2,1,0:T(8,128)}, f32[8,8,64,256]{3,2,1,0:T(8,128)S(1)}, u32[]{:S(2)}) copy-start(f32[8,8,64,256]{3,2,1,0:T(8,128)S(1)} %fusion.42) | copy-start | bytes 12582916
  429.0 197.9 %all-gather.7.cloned.1.call-start = ((), (), s32[]{:S(2)}) async-start(), calls=%async_computation.7 | async-start | bytes 17039360 | tf_op jit(solution)/shard_map/all_gather | solution.py:15
  432.1 15.6 %all-to-all-start.4 = ((bf16[128,4,1024]{2,0,1:T(8,128)(2,1)}), bf16[128,4,1024]{2,0,1:T(8,128)(2,1)S(1)}, u32[]{:S(2)}, u32[]{:S(2)}) async-start(bf16[128,4,1024]{2,0,1:T(8,128)(2,1)} %bitcast.204), calls=%async_computation.4 | async-start | bytes 2097152 | tf_op jit(solution)/shard_map/all_to_all | solution.py:70
  449.2 3.0 copy-start.2
  799.2 5.3 copy-start.9
  800.5 18.8 %all-to-all-start.5 = ((bf16[4,128,1024]{2,1,0:T(8,128)(2,1)}), bf16[4,128,1024]{2,1,0:T(8,128)(2,1)S(1)}, u32[]{:S(2)}, u32[]{:S(2)}) async-start(bf16[4,128,1024]{2,1,0:T(8,128)(2,1)} %convert_element_type.136), calls=%async_computation.5 | async-start | bytes 2097152 | tf_op jit(solution)/shard_map/all_to_all | solution.py:178
  824.6 2.0 copy-start.6
Sparse Core Ops, SparseCore 0:
  429.1 98.6 all-gather.4
  530.6 96.2 all-gather.6
where the time goes:
time: 841 us; the launch traced here: 838 us
  other arithmetic  337 us (40%)
  matrix products  214 us (25%)
  waiting for transfers between devices  210 us (25%)
  local copies, waits for them, and re-layouts  34.2 us (4%)
  starting transfers between devices  25.2 us (3%)
  between operations  13.7 us (2%)
    another operation x2, other arithmetic, body(): jax.scipy.linalg.solve_triangular(jnp.eye(C, dtype=jnp.float32) + lower_p...  315 us
    all_gather x2, waiting for transfers between devices, carried_in(): lax.all_gather(a.astype(kind), axis)  173 us
    dot_general x63, matrix products, compose(): jnp.einsum('hde,hef->hdf', later[0], earlier[1], precision=PRECISE)  91.3 us
  transfers between devices with their start and end apart: 8, of which 5 were waited for; matrix products, arithmetic and copies ran while one was open for 41% of the time, Pallas kernels for 0%

commit v1 on v0

v1 whole, which is shorter than its diff:
```python
import jax
import jax.numpy as jnp
from jax import lax
from jax.experimental import pallas as pl
from jax.experimental.pallas import tpu as pltpu
from jax.sharding import PartitionSpec as P

MESH = pl.DeviceIdType.MESH
F32 = jnp.float32
BF16 = jnp.bfloat16
HEADS = 32
T = 128
SLAB = 32
ZN = 8
BATCH = 4


def mm(a, b):
    return jnp.dot(a, b, preferred_element_type=F32)


def mmb(a, b):
    return mm(a.astype(BF16), b.astype(BF16))


def split(a):
    hi = a.astype(BF16)
    return hi, (a - hi.astype(F32)).astype(BF16)


def mm3(a, b):
    ah, al = split(a)
    bh, bl = split(b)
    first = mm(jnp.concatenate([ah, al], axis=1), jnp.concatenate([bh, bh], axis=0))
    return first + mm(ah, bl)


def mm_exact(a, b):
    bh, bl = split(b)
    return mm(jnp.concatenate([a, a], axis=1), jnp.concatenate([bh, bl], axis=0))


def bias_kernel(own_ref, out_ref, got, send_sem, recv_sem):
    ctx = lax.axis_index("context")
    hd = lax.axis_index("head")
    barrier = pltpu.get_barrier_semaphore()
    for s in range(1, 4):
        pl.semaphore_signal(
            barrier, inc=1, device_id=(ctx, lax.rem(hd + s, 4)), device_id_type=MESH
        )
    pl.semaphore_wait(barrier, 3)
    copies = []
    for s in range(1, 4):
        copy = pltpu.make_async_remote_copy(
            src_ref=own_ref,
            dst_ref=got.at[s - 1],
            send_sem=send_sem.at[s - 1],
            recv_sem=recv_sem.at[s - 1],
            device_id=(ctx, lax.rem(hd + s, 4)),
            device_id_type=MESH,
        )
        copy.start()
        copies.append(copy)
    for copy in copies:
        copy.wait()
    out_ref[...] = own_ref[...] + got[0] + got[1] + got[2]


def all_biases(decay_bias):
    hd = lax.axis_index("head")
    lanes = lax.broadcasted_iota(jnp.int32, (8, 128), 1)
    tiled = jnp.tile(decay_bias, 16)[None, :]
    own = jnp.where(lanes // 8 == hd, tiled, 0.0)
    vmem = pl.BlockSpec(memory_space=pltpu.VMEM)
    return pl.pallas_call(
        bias_kernel,
        out_shape=jax.ShapeDtypeStruct((8, 128), F32),
        in_specs=[vmem],
        out_specs=vmem,
        scratch_shapes=[
            pltpu.VMEM((3, 8, 128), F32),
            pltpu.SemaphoreType.DMA((3,)),
            pltpu.SemaphoreType.DMA((3,)),
        ],
        compiler_params=pltpu.CompilerParams(collective_id=0, has_side_effects=True),
    )(own)


def local_kernel(
    doc_ref, bias_ref, decay_ref, beta_ref, q_ref, k_ref, v_ref,
    ab_ref, r_ref, l_ref,
    pad, row_g, col_g, col_b, masks,
):
    step = pl.program_id(0)
    hd = lax.axis_index("head")
    keep0 = 1.0 - doc_ref[2 * hd].astype(F32)
    keep1 = 1.0 - doc_ref[2 * hd + 1].astype(F32)
    rows = lax.broadcasted_iota(jnp.int32, (T, T), 0)
    cols = lax.broadcasted_iota(jnp.int32, (T, T), 1)

    @pl.when(step == 0)
    def _():
        x = decay_ref[...] + bias_ref[0:1, 0:HEADS]
        tail = jnp.exp(-jnp.abs(x))
        one = 1.0 + tail
        away = one - 1.0
        exact = away == 0.0
        log1p = jnp.where(exact, tail, jnp.log(one) * (tail / jnp.where(exact, 1.0, away)))
        pad[...] = jnp.zeros((T, T), F32)
        pad[:, 0:HEADS] = -(jnp.maximum(x, 0.0) + log1p)
        lower = jnp.where(rows >= cols, 1.0, 0.0).astype(F32)
        cum = jnp.dot(
            lower, pad[...], preferred_element_type=F32, precision=lax.Precision.HIGHEST
        )
        row_g[...] = cum.T
        beta = 1.0 / (1.0 + jnp.exp(-beta_ref[...]))
        for h in range(HEADS):
            col_g[h] = jnp.broadcast_to(cum[:, h : h + 1], (T, T))
            col_b[h] = jnp.broadcast_to(beta[:, h : h + 1], (T, T))
        crossing = jnp.where((rows >= 64) & (cols < 64), keep1, 1.0)
        masks[0] = jnp.where(rows >= cols, crossing, 0.0)
        masks[1] = keep0 * jnp.where(rows >= 64, keep1, 1.0)
        masks[2] = jnp.where(cols >= 64, 1.0, keep1)

    inclusive = masks[0]
    reach = masks[1]
    leave = masks[2]

    def one_head(j):
        h = step * BATCH + j
        lanes = slice(j * 128, (j + 1) * 128)
        raw = k_ref[:, lanes].astype(F32)
        total = jnp.sum(raw * raw, axis=-1, keepdims=True)
        kf = (raw * lax.rsqrt(total + 1e-06)).astype(BF16).astype(F32)
        kt = kf.T
        kn = kf.astype(BF16)
        q = q_ref[:, lanes]
        cg = col_g[h]
        rg = row_g[pl.ds(h, 1), :]
        bt = col_b[h]
        decay = jnp.exp(jnp.minimum(cg - rg, 0.0)) * inclusive
        grams = mm(jnp.concatenate([kn, q], axis=0), kt.astype(BF16))
        low = jnp.where(rows > cols, bt * decay * grams[:T], 0.0)
        mix = decay * grams[T:]
        parts = []
        for b in range(16):
            block = low[8 * b : 8 * b + 8, :]
            x = jnp.where(rows[:8] + 8 * b == cols[:8], 1.0, 0.0).astype(F32)
            for c in range(7):
                x = x - block[:, 8 * b + c : 8 * b + c + 1] * x[c : c + 1, :]
            parts.append(x)
        x = jnp.concatenate(parts, axis=0)
        for small, large in ((8, 32), (32, 128)):
            off = (rows // small != cols // small) & (rows // large == cols // large)
            n = mmb(x, jnp.where(off, low, 0.0))
            nb = n.astype(BF16)
            y = x - mmb(nb, x)
            x = y + mmb(mm(nb, nb), y)
        e = jnp.exp(cg) * reach
        rhs = jnp.concatenate(
            [(bt * e * kf).astype(BF16), (bt * v_ref[:, lanes].astype(F32)).astype(BF16)], axis=1
        )
        wu = mmb(x, rhs).astype(BF16)
        last = cg[T - 1 : T, :]
        ends = kt * (jnp.exp(last - rg) * leave[0:1, :])
        both = mm(jnp.concatenate([mix.astype(BF16), ends.astype(BF16)], axis=0), wu)
        r_ref[j] = (e * q.astype(F32) - both[:T, :128]).astype(BF16)
        l_ref[j] = both[:T, 128:].astype(BF16)
        diag = jnp.where(rows == cols, 1.0 - jnp.exp(last) * (keep0 * keep1), 0.0)
        ab_ref[j, 0] = (diag + both[T:, :128]).astype(BF16)
        ab_ref[j, 1] = both[T:, 128:].astype(BF16)

    for j in range(BATCH):
        one_head(j)


def local_part(doc_start, biases, decay_logit, beta_logit, queries, key_input, value_input):
    wide = pl.BlockSpec((T, BATCH * 128), lambda g: (0, g))
    whole = lambda shape: pl.BlockSpec(shape, lambda g: (0,) * len(shape))
    head = pl.BlockSpec((BATCH, T, 128), lambda g: (g, 0, 0))
    return pl.pallas_call(
        local_kernel,
        grid=(HEADS // BATCH,),
        in_specs=[
            pl.BlockSpec(memory_space=pltpu.SMEM),
            whole((8, 128)), whole((T, HEADS)), whole((T, HEADS)),
            wide, wide, wide,
        ],
        out_specs=(pl.BlockSpec((BATCH, 2, 128, 128), lambda g: (g, 0, 0, 0)), head, head),
        out_shape=(
            jax.ShapeDtypeStruct((HEADS, 2, 128, 128), BF16),
            jax.ShapeDtypeStruct((HEADS, T, 128), BF16),
            jax.ShapeDtypeStruct((HEADS, T, 128), BF16),
        ),
        scratch_shapes=[
            pltpu.VMEM((T, T), F32),
            pltpu.VMEM((T, T), F32),
            pltpu.VMEM((HEADS, T, T), F32),
            pltpu.VMEM((HEADS, T, T), F32),
            pltpu.VMEM((3, T, T), F32),
        ],
        compiler_params=pltpu.CompilerParams(dimension_semantics=("arbitrary",)),
    )(doc_start, biases, decay_logit, beta_logit, queries, key_input, value_input)


def scan_kernel(
    ab_ref, out_ref,
    got, cur, pre_a, pre_b, blocks, zown, zgot, entry, stage,
    s1, r1, sz, rz, s3, r3,
):
    ctx = lax.axis_index("context")
    hd = lax.axis_index("head")
    z = ctx // 8
    xc = lax.rem(ctx, 8)
    me = xc * 4 + hd

    def peer(i):
        return (z * 8 + i // 4, lax.rem(i, 4))

    def zpeer(i):
        return (i * 8 + xc, hd)

    barrier = pltpu.get_barrier_semaphore()

    def greet(s, _):
        pl.semaphore_signal(
            barrier, inc=1, device_id=peer(lax.rem(me + s, SLAB)), device_id_type=MESH
        )
        return 0

    def zgreet(s, _):
        pl.semaphore_signal(
            barrier, inc=1, device_id=zpeer(lax.rem(z + s, ZN)), device_id_type=MESH
        )
        return 0

    lax.fori_loop(1, SLAB, greet, 0)
    lax.fori_loop(1, ZN, zgreet, 0)
    pl.semaphore_wait(barrier, SLAB - 1 + ZN - 1)

    def out_copy(i, slot):
        return pltpu.make_async_remote_copy(
            src_ref=ab_ref.at[i], dst_ref=got.at[slot],
            send_sem=s1.at[i], recv_sem=r1.at[slot],
            device_id=peer(i), device_id_type=MESH,
        )

    def z_copy(i, slot):
        return pltpu.make_async_remote_copy(
            src_ref=zown, dst_ref=zgot.at[slot],
            send_sem=sz.at[i], recv_sem=rz.at[slot],
            device_id=zpeer(i), device_id_type=MESH,
        )

    def back_copy(i, slot):
        return pltpu.make_async_remote_copy(
            src_ref=stage.at[i], dst_ref=out_ref.at[slot],
            send_sem=s3.at[i], recv_sem=r3.at[slot],
            device_id=peer(i), device_id_type=MESH,
        )

    def others(n, mine, act):
        def body(s, _):
            act(lax.rem(mine + s, n))
            return 0

        lax.fori_loop(1, n, body, 0)

    others(SLAB, me, lambda i: out_copy(i, me).start())
    got[me] = ab_ref[me]
    others(SLAB, me, lambda i: out_copy(i, i).wait_recv())

    eye = jnp.where(
        lax.broadcasted_iota(jnp.int32, (128, 128), 0)
        == lax.broadcasted_iota(jnp.int32, (128, 128), 1),
        1.0, 0.0,
    ).astype(BF16)
    for j in range(4):
        pre_a[8 * j] = jnp.concatenate([eye, jnp.zeros((128, 128), BF16)], axis=1)
        pre_b[8 * j] = jnp.zeros((128, 128), F32)
        cur[j, :, :128] = eye.astype(F32) - got[8 * j, 0].astype(F32)
        cur[j, :, 128:] = got[8 * j, 1].astype(F32)

    def extend(i, _):
        for j in range(4):
            now = cur[j]
            hi, lo = split(now)
            pre_a[8 * j + i] = jnp.concatenate([hi[:, :128], lo[:, :128]], axis=1)
            pre_b[8 * j + i] = now[:, 128:]
            a = got[8 * j + i, 0]
            b = got[8 * j + i, 1].astype(F32)
            new = now - mm(jnp.concatenate([a, a], axis=1), jnp.concatenate([hi, lo], axis=0))
            cur[j] = jnp.concatenate([new[:, :128], new[:, 128:] + b], axis=1)
        return 0

    lax.fori_loop(1, 8, extend, 0)

    def compose(later, earlier):
        new = mm3(later[:, :128], earlier)
        return jnp.concatenate([new[:, :128], new[:, 128:] + later[:, 128:]], axis=1)

    blocks[0] = cur[0]
    blocks[1] = compose(cur[1], blocks[0])
    blocks[2] = compose(cur[2], blocks[1])
    total = compose(cur[3], blocks[2])
    zown[0] = (eye.astype(F32) - total[:, :128]).astype(BF16)
    zown[1] = total[:, 128:].astype(BF16)
    others(ZN, z, lambda i: z_copy(i, z).start())
    entry[...] = jnp.zeros((128, 128), F32)
    others(ZN, z, lambda i: z_copy(i, i).wait_recv())

    def carry(i, _):
        before = entry[...]
        entry[...] = before - mm_exact(zgot[i, 0], before) + zgot[i, 1].astype(F32)
        return 0

    lax.fori_loop(0, z, carry, 0)

    first = entry[...]
    starts = [first]
    for j in range(3):
        starts.append(mm3(blocks[j][:, :128], first) + blocks[j][:, 128:])
    for j in range(4):
        hi = starts[j].astype(BF16)
        cur[j, :, :128] = hi.astype(F32)

    def spread(g):
        for c in range(4):
            i = lax.rem(me + 4 * g + c, SLAB)
            hi = cur[i // 8, :, :128].astype(BF16)
            value = mm(pre_a[i], jnp.concatenate([hi, hi], axis=0)) + pre_b[i]
            stage[i] = value.astype(BF16)

    def deliver(g, least):
        for c in range(least, 4):
            i = lax.rem(me + 4 * g + c, SLAB)
            back_copy(i, me).start()

    spread(0)
    spread(1)
    deliver(0, 1)

    def rest(g, _):
        spread(g)
        deliver(g - 1, 0)
        return 0

    lax.fori_loop(2, 8, rest, 0)
    out_ref[me] = stage[me]
    deliver(7, 0)
    others(SLAB, me, lambda i: back_copy(i, i).wait_recv())
    others(SLAB, me, lambda i: out_copy(i, me).wait_send())
    others(ZN, z, lambda i: z_copy(i, z).wait_send())
    others(SLAB, me, lambda i: back_copy(i, me).wait_send())


def entering_states(ab):
    vmem = pl.BlockSpec(memory_space=pltpu.VMEM)
    dma = pltpu.SemaphoreType.DMA
    return pl.pallas_call(
        scan_kernel,
        out_shape=jax.ShapeDtypeStruct((HEADS, 128, 128), BF16),
        in_specs=[vmem],
        out_specs=vmem,
        scratch_shapes=[
            pltpu.VMEM((SLAB, 2, 128, 128), BF16),
            pltpu.VMEM((4, 128, 256), F32),
            pltpu.VMEM((SLAB, 128, 256), BF16),
            pltpu.VMEM((SLAB, 128, 128), F32),
            pltpu.VMEM((3, 128, 256), F32),
            pltpu.VMEM((2, 128, 128), BF16),
            pltpu.VMEM((ZN, 2, 128, 128), BF16),
            pltpu.VMEM((128, 128), F32),
            pltpu.VMEM((SLAB, 128, 128), BF16),
            dma((SLAB,)), dma((SLAB,)), dma((ZN,)), dma((ZN,)), dma((SLAB,)), dma((SLAB,)),
        ],
        compiler_params=pltpu.CompilerParams(collective_id=1, has_side_effects=True),
    )(ab)


def out_kernel(gain_ref, r_ref, l_ref, s_ref, gate_ref, o_ref):
    gain = gain_ref[0:1, :]
    for j in range(BATCH):
        lanes = slice(j * 128, (j + 1) * 128)
        core = (l_ref[j].astype(F32) + mm(r_ref[j], s_ref[j])).astype(BF16).astype(F32)
        mean = jnp.sum(core * core, axis=-1, keepdims=True) * (1.0 / 128)
        gate = gate_ref[:, lanes].astype(F32)
        silu = gate / (1.0 + jnp.exp(-gate))
        o_ref[:, lanes] = (core * lax.rsqrt(mean + 1e-06) * gain * silu).astype(BF16)


def outputs(norm_gain, r, lo, states, gate_input):
    wide = pl.BlockSpec((T, BATCH * 128), lambda g: (0, g))
    head = pl.BlockSpec((BATCH, T, 128), lambda g: (g, 0, 0))
    return pl.pallas_call(
        out_kernel,
        grid=(HEADS // BATCH,),
        in_specs=[pl.BlockSpec((1, 128), lambda g: (0, 0)), head, head, head, wide],
        out_specs=wide,
        out_shape=jax.ShapeDtypeStruct(gate_input.shape, BF16),
        compiler_params=pltpu.CompilerParams(dimension_semantics=("arbitrary",)),
    )(norm_gain[None, :], r, lo, states, gate_input)


def body(
    queries, key_input, value_input, gate_input,
    decay_logit, beta_logit, decay_bias, norm_gain, doc_start,
):
    biases = all_biases(decay_bias)
    ab, r, lo = local_part(
        doc_start, biases, decay_logit, beta_logit, queries, key_input, value_input
    )
    states = entering_states(ab)
    return outputs(norm_gain, r, lo, states, gate_input)


def solution(mesh):
    rows = P(("context", "head"), None)
    return jax.shard_map(
        body,
        mesh=mesh,
        in_specs=(rows, rows, rows, rows, rows, rows, P("head"), P(), P("context")),
        out_specs=rows,
        check_vma=False,
    )
```

time: 841 us -> 136 us (0.16)
  the two profiles are of different devices: /device:TPU:231 before, /device:TPU:1 now
where the time goes in v1:
time: 136 us; the launch traced here: 135 us
  Pallas kernels  131 us (96%)
  local copies, waits for them, and re-layouts  3.64 us (3%)
    pallas_call x1, Pallas kernels, entering_states(): pl.pallas_call(scan_kernel, out_shape=jax.ShapeDtypeStruct((HEADS, 128, 1...  72.5 us
    pallas_call x1, Pallas kernels, local_part(): pl.pallas_call(local_kernel, grid=(HEADS // BATCH,), in_specs=[pl.BlockSp...  44.5 us
    pallas_call x1, Pallas kernels, all_biases(): pl.pallas_call(bias_kernel, out_shape=jax.ShapeDtypeStruct((8, 128), F32)...  7.1 us
    pallas_call x1, Pallas kernels, outputs(): pl.pallas_call(out_kernel, grid=(HEADS // BATCH,), in_specs=[pl.BlockSpec...  7.02 us
    unnamed x2, local copies, waits for them, and re-layouts  2.9 us

profile of v1, /device:TPU:1, one launch (start us, length us, event | category | flops | bytes accessed | tf_op | source)
XLA Modules:
  0.0 135.5 jit_solution(16060216578155149250)
XLA Ops:
  0.0 0.7 tile.2
  0.7 0.1 broadcast_in_dim.18
  0.8 0.6 fusion.own_ref
  1.4 7.1 %shard_map.91.bias_ref = f32[8,128]{1,0:T(8,128)} custom-call(f32[8,128]{1,0:T(8,128)} %fusion.own_ref), custom_call_target="tpu_custom_call" | custom-call | tf_op jit(solution)/shard_map/pallas_call | solution.py:75
  8.5 1.4 %copy.12.decay_ref = f32[128,32]{1,0:T(8,128)} copy(f32[128,32]{0,1:T(8,128)} %param.13) | data formatting | bytes 32768 | tf_op args[4]
  9.9 1.4 %copy.13.beta_ref = f32[128,32]{1,0:T(8,128)} copy(f32[128,32]{0,1:T(8,128)} %param.14) | data formatting | bytes 32768 | tf_op args[5]
  11.4 44.5 %shard_map.92 = (bf16[32,2,128,128]{3,2,1,0:T(8,128)(2,1)}, bf16[32,128,128]{2,1,0:T(8,128)(2,1)}, bf16[32,128,128]{2,1,0:T(8,128)(2,1)}) custom-call(s32[8]{0:T(128)} %doc_ref.1, f32[8,128]{1,0:T(8,128)} %shard_map.91.bias_ref, f32[128,32]{1,0:T(8,128)} %copy.12.decay_ref, f32[128,32]{1,0:T(8,128)} %copy.13.beta_ref, bf16[128,4096]{1,0:T(8,128)(2,1)} %q_ref.1, ...), custom_call_target="tpu_custom_call" | custom-call | tf_op jit(solution)/shard_map/pallas_call | solution.py:181
  55.9 72.5 %shard_map.93.s_ref = bf16[32,128,128]{2,1,0:T(8,128)(2,1)} custom-call(bf16[32,2,128,128]{3,2,1,0:T(8,128)(2,1)} %get-tuple-element.10.ab_ref), custom_call_target="tpu_custom_call" | custom-call | tf_op jit(solution)/shard_map/pallas_call | solution.py:360
  128.5 7.0 %shard_map.94 = bf16[128,4096]{1,0:T(8,128)(2,1)} custom-call(f32[1,128]{1,0:T(1,128)} %bitcast.1, bf16[32,128,128]{2,1,0:T(8,128)(2,1)} %get-tuple-element.8.r_ref, bf16[32,128,128]{2,1,0:T(8,128)(2,1)} %get-tuple-element.9.l_ref, bf16[32,128,128]{2,1,0:T(8,128)(2,1)} %shard_map.93.s_ref, bf16[128,4096]{1,0:T(8,128)(2,1)} %gate_ref.1), custom_call_target="tpu_custom_call" | custom-call | tf_op jit(solution)/shard_map/pallas_call | solution.py:395
  (2 shorter events, 0.0 us)

commit v2 on v1

v2 whole, which is shorter than its diff:
```python
import jax
import jax.numpy as jnp
from jax import lax
from jax.experimental import pallas as pl
from jax.experimental.pallas import tpu as pltpu
from jax.sharding import PartitionSpec as P

MESH = pl.DeviceIdType.MESH
F32 = jnp.float32
BF16 = jnp.bfloat16
HEADS = 32
T = 128
SLAB = 32
ZN = 8
BATCH = 4
EARLY = 3


def mm(a, b):
    return jnp.dot(a, b, preferred_element_type=F32)


def mmb(a, b):
    return mm(a.astype(BF16), b.astype(BF16))


def split(a):
    hi = a.astype(BF16)
    return hi, (a - hi.astype(F32)).astype(BF16)


def mm3(a, b):
    ah, al = split(a)
    bh, bl = split(b)
    first = mm(jnp.concatenate([ah, al], axis=1), jnp.concatenate([bh, bh], axis=0))
    return first + mm(ah, bl)


def mm_exact(a, b):
    bh, bl = split(b)
    return mm(jnp.concatenate([a, a], axis=1), jnp.concatenate([bh, bl], axis=0))


def off_block(rows, cols, small, large):
    return (rows // small != cols // small) & (rows // large == cols // large)


def inverse8(low, rows, cols):
    block = jnp.where(rows // 8 == cols // 8, low, 0.0)
    x = jnp.where(rows == cols, 1.0, 0.0).astype(F32).reshape(16, 8, T)
    for c in range(7):
        factor = jnp.sum(jnp.where(cols % 8 == c, block, 0.0), axis=1, keepdims=True)
        x = x - factor.reshape(16, 8, 1) * x[:, c : c + 1, :]
    return x.reshape(T, T)


def diagonal(m):
    zero = jnp.zeros((T, T), BF16)
    top = jnp.concatenate([m[:, :T], zero], axis=1)
    return jnp.concatenate([top, jnp.concatenate([zero, m[:, T:]], axis=1)], axis=0)


def invert_pair(low_a, low_b, rows, cols):
    x = jnp.concatenate([inverse8(low_a, rows, cols), inverse8(low_b, rows, cols)], axis=1)
    for small, large in ((8, 32), (32, 128)):
        off = off_block(rows, cols, small, large)
        low = jnp.concatenate(
            [jnp.where(off, low_a, 0.0).astype(BF16), jnp.where(off, low_b, 0.0).astype(BF16)],
            axis=1,
        )
        xb = x.astype(BF16)
        n = mm(xb, diagonal(low)).astype(BF16)
        y = x - mm(n, diagonal(xb))
        x = y + mm(mm(n, diagonal(n)).astype(BF16), diagonal(y.astype(BF16)))
    return x[:, :T], x[:, T:]


def layer_kernel(
    doc_ref, own_bias, decay_ref, beta_ref, gain_ref, q_hbm, k_hbm, v_hbm, gate_hbm,
    o_ref,
    q_ref, k_ref, v_ref, gate_ref, bias, pad, row_g, col_g, col_b, masks,
    kts, wus, rs, ls,
    ab_ref, got, cur, pre_a, pre_b, blocks, zown, zgot, entry, stage, arrived,
    sin, sb, rb, s1, r1, sz, rz, s3, r3,
):
    ctx = lax.axis_index("context")
    hd = lax.axis_index("head")
    z = ctx // 8
    xc = lax.rem(ctx, 8)
    me = xc * 4 + hd

    loads = [
        pltpu.make_async_copy(a, b, sin.at[n])
        for n, (a, b) in enumerate(
            ((k_hbm, k_ref), (v_hbm, v_ref), (q_hbm, q_ref), (gate_hbm, gate_ref))
        )
    ]
    for load in loads:
        load.start()

    def peer(i):
        return (z * 8 + i // 4, lax.rem(i, 4))

    def zpeer(i):
        return (i * 8 + xc, hd)

    def others(n, mine, act):
        def step(s, _):
            act(lax.rem(mine + s, n))
            return 0

        lax.fori_loop(1, n, step, 0)

    barrier = pltpu.get_barrier_semaphore()

    def greet(device):
        pl.semaphore_signal(barrier, inc=1, device_id=device, device_id_type=MESH)

    others(SLAB, me, lambda i: greet(peer(i)))
    others(ZN, z, lambda i: greet(zpeer(i)))
    pl.semaphore_wait(barrier, SLAB - 1 + ZN - 1)

    def remote(src, dst, send, recv, device):
        return pltpu.make_async_remote_copy(
            src_ref=src, dst_ref=dst, send_sem=send, recv_sem=recv,
            device_id=device, device_id_type=MESH,
        )

    def bias_copy(i, slot):
        return remote(own_bias, bias.at[slot], sb.at[i], rb.at[slot], (ctx, i))

    def out_copy(i, slot):
        return remote(ab_ref.at[i], got.at[slot], s1.at[i], r1.at[slot], peer(i))

    def z_copy(i, slot):
        return remote(zown, zgot.at[slot], sz.at[i], rz.at[slot], zpeer(i))

    def back_copy(i, slot):
        return remote(stage.at[i], arrived.at[slot], s3.at[i], r3.at[slot], peer(i))

    others(4, hd, lambda i: bias_copy(i, hd).start())
    bias[hd] = own_bias[...]

    rows = lax.broadcasted_iota(jnp.int32, (T, T), 0)
    cols = lax.broadcasted_iota(jnp.int32, (T, T), 1)
    keep0 = 1.0 - doc_ref[2 * hd].astype(F32)
    keep1 = 1.0 - doc_ref[2 * hd + 1].astype(F32)
    masks[0] = jnp.where(rows >= cols, jnp.where((rows >= 64) & (cols < 64), keep1, 1.0), 0.0)
    masks[1] = keep0 * jnp.where(rows >= 64, keep1, 1.0)
    masks[2] = jnp.where(cols >= 64, 1.0, keep1)
    pad[HEADS : 2 * HEADS] = 1.0 / (1.0 + jnp.exp(-beta_ref[...]))
    pad[2 * HEADS :] = jnp.zeros((2 * HEADS, T), F32)

    others(4, hd, lambda i: bias_copy(i, i).wait_recv())
    x = decay_ref[...] + bias[...].reshape(HEADS, T)
    tail = jnp.exp(-jnp.abs(x))
    one = 1.0 + tail
    away = one - 1.0
    exact = away == 0.0
    log1p = jnp.where(exact, tail, jnp.log(one) * (tail / jnp.where(exact, 1.0, away)))
    upper = jnp.where(rows <= cols, 1.0, 0.0).astype(F32)
    cum = jnp.dot(
        -(jnp.maximum(x, 0.0) + log1p), upper,
        preferred_element_type=F32, precision=lax.Precision.HIGHEST,
    )
    row_g[...] = cum
    pad[0:HEADS] = cum
    by_token = pad[...].T
    for h in range(HEADS):
        col_g[h] = jnp.broadcast_to(by_token[:, h : h + 1], (T, T))
        col_b[h] = jnp.broadcast_to(by_token[:, HEADS + h : HEADS + h + 1], (T, T))

    loads[0].wait()
    loads[1].wait()

    def lanes_of(h):
        return pl.ds(pl.multiple_of(h * 128, 128), 128)

    def decay_of(h):
        gap = col_g[h] - row_g[pl.ds(h, 1), :]
        return jnp.exp(jnp.minimum(gap, 0.0)) * masks[0]

    def maps(g, _):
        @pl.when(g > 0)
        def _():
            for c in range(BATCH):
                i = lax.rem(me + 1 + BATCH * (g - 1) + c, SLAB)
                out_copy(i, me).start()

        heads = [lax.rem(me + 1 + BATCH * g + c, SLAB) for c in range(BATCH)]
        lows, keys, turned = [], [], []
        for h in heads:
            raw = k_ref[:, lanes_of(h)].astype(F32)
            total = jnp.sum(raw * raw, axis=-1, keepdims=True)
            kn = (raw * lax.rsqrt(total + 1e-06)).astype(BF16)
            kf = kn.astype(F32)
            kt = kf.T
            kb = kt.astype(BF16)
            kts[h] = kb
            low = jnp.where(rows > cols, col_b[h] * decay_of(h) * mm(kn, kb), 0.0)
            lows.append(low)
            keys.append(kf)
            turned.append(kt)
        inverses = []
        for c in range(0, BATCH, 2):
            inverses += list(invert_pair(lows[c], lows[c + 1], rows, cols))
        for c, h in enumerate(heads):
            bt = col_b[h]
            e = jnp.exp(col_g[h]) * masks[1]
            rhs = jnp.concatenate(
                [
                    (bt * e * keys[c]).astype(BF16),
                    (bt * v_ref[:, lanes_of(h)].astype(F32)).astype(BF16),
                ],
                axis=1,
            )
            wu = mmb(inverses[c], rhs).astype(BF16)
            wus[h] = wu
            rg = row_g[pl.ds(h, 1), :]
            last = col_g[h, T - 1 : T, :]
            ends = turned[c] * (jnp.exp(last - rg) * masks[2, 0:1, :])
            both = mm(ends.astype(BF16), wu)
            diag = jnp.where(rows == cols, 1.0 - jnp.exp(last) * (keep0 * keep1), 0.0)
            ab_ref[h, 0] = (diag + both[:, :128]).astype(BF16)
            ab_ref[h, 1] = both[:, 128:].astype(BF16)
        return 0

    steps = HEADS // BATCH
    lax.fori_loop(0, steps, maps, 0)
    for c in range(BATCH - 1):
        out_copy(lax.rem(me + 1 + BATCH * (steps - 1) + c, SLAB), me).start()
    got[me] = ab_ref[me]

    def reads(g, _):
        for c in range(4):
            h = 4 * g + c
            q = q_ref[:, lanes_of(h)]
            mix = decay_of(h) * mm(q, kts[h])
            both = mmb(mix, wus[h])
            e = jnp.exp(col_g[h]) * masks[1]
            rs[h] = (e * q.astype(F32) - both[:, :128]).astype(BF16)
            ls[h] = both[:, 128:]
        return 0

    loads[2].wait()
    lax.fori_loop(0, EARLY, reads, 0)
    others(SLAB, me, lambda i: out_copy(i, i).wait_recv())

    eye = jnp.where(rows == cols, 1.0, 0.0).astype(F32)
    for j in range(4):
        pre_a[8 * j, :, :128] = eye.astype(BF16)
        pre_a[8 * j, :, 128:] = jnp.zeros((128, 128), BF16)
        pre_b[8 * j] = jnp.zeros((128, 128), F32)
        cur[j, :, :128] = eye - got[8 * j, 0].astype(F32)
        cur[j, :, 128:] = got[8 * j, 1].astype(F32)

    def extend(i, _):
        for j in range(4):
            now = cur[j]
            hi, lo = split(now)
            pre_a[8 * j + i] = jnp.concatenate([hi[:, :128], lo[:, :128]], axis=1)
            pre_b[8 * j + i] = now[:, 128:]
            a = got[8 * j + i, 0]
            b = got[8 * j + i, 1].astype(F32)
            new = now - mm(jnp.concatenate([a, a], axis=1), jnp.concatenate([hi, lo], axis=0))
            cur[j] = jnp.concatenate([new[:, :128], new[:, 128:] + b], axis=1)
        return 0

    lax.fori_loop(1, 8, extend, 0)

    def compose(later, earlier):
        new = mm3(later[:, :128], earlier)
        return jnp.concatenate([new[:, :128], new[:, 128:] + later[:, 128:]], axis=1)

    blocks[0] = cur[0]
    blocks[1] = compose(cur[1], blocks[0])
    blocks[2] = compose(cur[2], blocks[1])
    total = compose(cur[3], blocks[2])
    zown[0] = (eye - total[:, :128]).astype(BF16)
    zown[1] = total[:, 128:].astype(BF16)
    others(ZN, z, lambda i: z_copy(i, z).start())
    entry[...] = jnp.zeros((128, 128), F32)
    lax.fori_loop(EARLY, 8, reads, 0)
    others(ZN, z, lambda i: z_copy(i, i).wait_recv())

    def carry(i, _):
        before = entry[...]
        entry[...] = before - mm_exact(zgot[i, 0], before) + zgot[i, 1].astype(F32)
        return 0

    lax.fori_loop(0, z, carry, 0)

    first = entry[...]
    starts = [first]
    for j in range(3):
        starts.append(mm3(blocks[j][:, :128], first) + blocks[j][:, 128:])
    for j in range(4):
        cur[j, :, :128] = starts[j].astype(BF16).astype(F32)

    def spread(g):
        for c in range(4):
            i = lax.rem(me + 4 * g + c, SLAB)
            hi = cur[i // 8, :, :128].astype(BF16)
            value = mm(pre_a[i], jnp.concatenate([hi, hi], axis=0)) + pre_b[i]
            stage[i] = value.astype(BF16)

    def deliver(g, least):
        for c in range(least, 4):
            back_copy(lax.rem(me + 4 * g + c, SLAB), me).start()

    spread(0)
    spread(1)
    deliver(0, 1)

    def rest(g, _):
        spread(g)
        deliver(g - 1, 0)
        return 0

    lax.fori_loop(2, 8, rest, 0)
    arrived[me] = stage[me]
    deliver(7, 0)
    loads[3].wait()

    def finish(g, least):
        heads = [lax.rem(me + SLAB - (4 * g + c), SLAB) for c in range(4)]
        for i in heads[least:]:
            back_copy(i, i).wait_recv()
        for h in heads:
            core = (ls[h] + mm(rs[h], arrived[h])).astype(BF16).astype(F32)
            mean = jnp.sum(core * core, axis=-1, keepdims=True) * (1.0 / 128)
            gate = gate_ref[:, lanes_of(h)].astype(F32)
            silu = gate / (1.0 + jnp.exp(-gate))
            scaled = core * lax.rsqrt(mean + 1e-06) * gain_ref[...]
            o_ref[:, lanes_of(h)] = (scaled * silu).astype(BF16)

    finish(0, 1)

    def finish_rest(g, _):
        finish(g, 0)
        return 0

    lax.fori_loop(1, 8, finish_rest, 0)
    others(4, hd, lambda i: bias_copy(i, hd).wait_send())
    others(SLAB, me, lambda i: out_copy(i, me).wait_send())
    others(ZN, z, lambda i: z_copy(i, z).wait_send())
    others(SLAB, me, lambda i: back_copy(i, me).wait_send())


def body(
    queries, key_input, value_input, gate_input,
    decay_logit, beta_logit, decay_bias, norm_gain, doc_start,
):
    vmem = pl.BlockSpec(memory_space=pltpu.VMEM)
    hbm = pl.BlockSpec(memory_space=pl.ANY)
    dma = pltpu.SemaphoreType.DMA
    rows = pltpu.VMEM((T, HEADS * 128), BF16)
    square = pltpu.VMEM((T, T), F32)
    return pl.pallas_call(
        layer_kernel,
        out_shape=jax.ShapeDtypeStruct(gate_input.shape, BF16),
        in_specs=[pl.BlockSpec(memory_space=pltpu.SMEM)] + [vmem] * 4 + [hbm] * 4,
        out_specs=vmem,
        scratch_shapes=[
            rows, rows, rows, rows,
            pltpu.VMEM((4, 8, T), F32),
            square,
            pltpu.VMEM((HEADS, T), F32),
            pltpu.VMEM((HEADS, T, T), F32),
            pltpu.VMEM((HEADS, T, T), F32),
            pltpu.VMEM((3, T, T), F32),
            pltpu.VMEM((HEADS, 128, T), BF16),
            pltpu.VMEM((HEADS, T, 256), BF16),
            pltpu.VMEM((HEADS, T, 128), BF16),
            pltpu.VMEM((HEADS, T, 128), F32),
            pltpu.VMEM((HEADS, 2, 128, 128), BF16),
            pltpu.VMEM((SLAB, 2, 128, 128), BF16),
            pltpu.VMEM((4, 128, 256), F32),
            pltpu.VMEM((SLAB, 128, 256), BF16),
            pltpu.VMEM((SLAB, 128, 128), F32),
            pltpu.VMEM((3, 128, 256), F32),
            pltpu.VMEM((2, 128, 128), BF16),
            pltpu.VMEM((ZN, 2, 128, 128), BF16),
            pltpu.VMEM((128, 128), F32),
            pltpu.VMEM((SLAB, 128, 128), BF16),
            pltpu.VMEM((SLAB, 128, 128), BF16),
            dma((4,)), dma((4,)), dma((4,)),
            dma((SLAB,)), dma((SLAB,)), dma((ZN,)), dma((ZN,)), dma((SLAB,)), dma((SLAB,)),
        ],
        compiler_params=pltpu.CompilerParams(collective_id=0, has_side_effects=True),
    )(
        doc_start,
        jnp.broadcast_to(decay_bias[:, None], (8, T)),
        decay_logit.T, beta_logit.T, norm_gain[None, :],
        queries, key_input, value_input, gate_input,
    )


def solution(mesh):
    rows = P(("context", "head"), None)
    return jax.shard_map(
        body,
        mesh=mesh,
        in_specs=(rows, rows, rows, rows, rows, rows, P("head"), P(), P("context")),
        out_specs=rows,
        check_vma=False,
    )
```

time: 136 us -> 90.7 us (0.67)
  Pallas kernels: 131 us -> 86.9 us
    pallas_call x4 -> x1, Pallas kernels: 131 us -> 86.9 us  [body(): pl.pallas_call(layer_kernel, out_shape=jax.ShapeDtypeStruct(gate_input.sh...]
    unnamed x2 -> x3, local copies, waits for them, and re-layouts: 2.9 us -> 2.94 us
where the time goes in v2:
time: 90.7 us; the launch traced here: 90.5 us
  Pallas kernels  86.9 us (96%)
  local copies, waits for them, and re-layouts  3.6 us (4%)
    pallas_call x1, Pallas kernels, body(): pl.pallas_call(layer_kernel, out_shape=jax.ShapeDtypeStruct(gate_input.sh...  86.9 us
    unnamed x3, local copies, waits for them, and re-layouts  2.94 us

profile of v2, /device:TPU:1, one launch (start us, length us, event | category | flops | bytes accessed | tf_op | source)
XLA Modules:
  0.0 90.5 jit_solution(14833233428451692818)
XLA Ops:
  0.0 0.0 copy-start
  0.0 0.7 copy-done
  0.7 0.7 broadcast_in_dim.4.own_bias
  1.3 86.9 %shard_map.91 = bf16[128,4096]{1,0:T(8,128)(2,1)} custom-call(s32[8]{0:T(128)} %doc_ref.1, f32[8,128]{1,0:T(8,128)} %broadcast_in_dim.4.own_bias, f32[32,128]{1,0:T(8,128)} %bitcast.3, f32[32,128]{1,0:T(8,128)} %bitcast.4, f32[1,128]{1,0:T(1,128)} %bitcast.5, bf16[128,4096]{1,0:T(8,128)(2,1)} %q_hbm.1, bf16[128,4096]{1,0:T(8,128)(2,1)} %k_hbm.1, ...), custom_call_target="tpu_custom_call" | custom-call | tf_op jit(solution)/shard_map/pallas_call | solution.py:359
  88.2 2.3 %copy.11 = bf16[128,4096]{1,0:T(8,128)(2,1)} copy(bf16[128,4096]{1,0:T(8,128)(2,1)} %shard_map.91) | data formatting | bytes 2097152
Async XLA Ops:
  0.0 0.7 copy-start

commit v3 on v2

--- a/solution.py
+++ b/solution.py
@@ -13,7 +13,8 @@
 SLAB = 32
 ZN = 8
 BATCH = 4
-EARLY = 3
+EARLY = 2
+STRIDE = 11
 
 
 def mm(a, b):
@@ -76,10 +77,10 @@
 
 
 def layer_kernel(
-    doc_ref, own_bias, decay_ref, beta_ref, gain_ref, q_hbm, k_hbm, v_hbm, gate_hbm,
+    doc_ref, bias_ref, decay_ref, beta_ref, gain_ref, q_hbm, k_hbm, v_hbm, gate_hbm,
     o_ref,
-    q_ref, k_ref, v_ref, gate_ref, bias, pad, row_g, col_g, col_b, masks,
-    kts, wus, rs, ls,
+    q_ref, k_ref, v_ref, gate_ref, own_bias, bias, gates, pad, tokens, row_g, col_g, col_b, masks,
+    kns, kts, wus, rs, ls,
     ab_ref, got, cur, pre_a, pre_b, blocks, zown, zgot, entry, stage, arrived,
     sin, sb, rb, s1, r1, sz, rz, s3, r3,
 ):
@@ -101,6 +102,9 @@
     def peer(i):
         return (z * 8 + i // 4, lax.rem(i, 4))
 
+    def turn(k):
+        return lax.rem(me + STRIDE * k, SLAB)
+
     def zpeer(i):
         return (i * 8 + xc, hd)
 
@@ -111,6 +115,13 @@
 
         lax.fori_loop(1, n, step, 0)
 
+    def later(act):
+        def step(i, _):
+            act(i)
+            return 0
+
+        lax.fori_loop(z + 1, ZN, step, 0)
+
     barrier = pltpu.get_barrier_semaphore()
 
     def greet(device):
@@ -118,7 +129,6 @@
 
     others(SLAB, me, lambda i: greet(peer(i)))
     others(ZN, z, lambda i: greet(zpeer(i)))
-    pl.semaphore_wait(barrier, SLAB - 1 + ZN - 1)
 
     def remote(src, dst, send, recv, device):
         return pltpu.make_async_remote_copy(
@@ -138,19 +148,37 @@
     def back_copy(i, slot):
         return remote(stage.at[i], arrived.at[slot], s3.at[i], r3.at[slot], peer(i))
 
-    others(4, hd, lambda i: bias_copy(i, hd).start())
-    bias[hd] = own_bias[...]
-
     rows = lax.broadcasted_iota(jnp.int32, (T, T), 0)
     cols = lax.broadcasted_iota(jnp.int32, (T, T), 1)
     keep0 = 1.0 - doc_ref[2 * hd].astype(F32)
     keep1 = 1.0 - doc_ref[2 * hd + 1].astype(F32)
+    for r in range(8):
+        own_bias[r : r + 1, :] = jnp.full((1, T), bias_ref[r], F32)
     masks[0] = jnp.where(rows >= cols, jnp.where((rows >= 64) & (cols < 64), keep1, 1.0), 0.0)
     masks[1] = keep0 * jnp.where(rows >= 64, keep1, 1.0)
     masks[2] = jnp.where(cols >= 64, 1.0, keep1)
-    pad[HEADS : 2 * HEADS] = 1.0 / (1.0 + jnp.exp(-beta_ref[...]))
+    gates[...] = 1.0 / (1.0 + jnp.exp(-beta_ref[...]))
     pad[2 * HEADS :] = jnp.zeros((2 * HEADS, T), F32)
 
+    pl.semaphore_wait(barrier, SLAB - 1 + ZN - 1)
+    others(4, hd, lambda i: bias_copy(i, hd).start())
+    bias[hd] = own_bias[...]
+
+    def lanes_of(h):
+        return pl.ds(pl.multiple_of(h * 128, 128), 128)
+
+    loads[0].wait()
+
+    def normalize(g):
+        for c in range(BATCH):
+            h = turn(1 + BATCH * g + c)
+            raw = k_ref[:, lanes_of(h)].astype(F32)
+            total = jnp.sum(raw * raw, axis=-1, keepdims=True)
+            kn = (raw * lax.rsqrt(total + 1e-06)).astype(BF16)
+            kns[h] = kn
+            kts[h] = kn.astype(F32).T.astype(BF16)
+
+    normalize(0)
     others(4, hd, lambda i: bias_copy(i, i).wait_recv())
     x = decay_ref[...] + bias[...].reshape(HEADS, T)
     tail = jnp.exp(-jnp.abs(x))
@@ -164,17 +192,13 @@
         preferred_element_type=F32, precision=lax.Precision.HIGHEST,
     )
     row_g[...] = cum
-    pad[0:HEADS] = cum
-    by_token = pad[...].T
-    for h in range(HEADS):
-        col_g[h] = jnp.broadcast_to(by_token[:, h : h + 1], (T, T))
-        col_b[h] = jnp.broadcast_to(by_token[:, HEADS + h : HEADS + h + 1], (T, T))
-
-    loads[0].wait()
+    for k in range(HEADS):
+        row = pl.ds(turn(k + 1), 1)
+        pad[k : k + 1] = row_g[row, :]
+        pad[HEADS + k : HEADS + k + 1] = gates[row, :]
+    tokens[...] = pad[...].T
+
     loads[1].wait()
-
-    def lanes_of(h):
-        return pl.ds(pl.multiple_of(h * 128, 128), 128)
 
     def decay_of(h):
         gap = col_g[h] - row_g[pl.ds(h, 1), :]
@@ -184,23 +208,20 @@
         @pl.when(g > 0)
         def _():
             for c in range(BATCH):
-                i = lax.rem(me + 1 + BATCH * (g - 1) + c, SLAB)
+                i = turn(1 + BATCH * (g - 1) + c)
                 out_copy(i, me).start()
 
-        heads = [lax.rem(me + 1 + BATCH * g + c, SLAB) for c in range(BATCH)]
-        lows, keys, turned = [], [], []
+        heads = [turn(1 + BATCH * g + c) for c in range(BATCH)]
+        normalize(g + 1)
+        lanes = tokens[...]
+        for c, h in enumerate(heads):
+            col_g[h] = jnp.broadcast_to(lanes[:, c : c + 1], (T, T))
+            col_b[h] = jnp.broadcast_to(lanes[:, HEADS + c : HEADS + c + 1], (T, T))
+        tokens[...] = jnp.concatenate([lanes[:, BATCH:], lanes[:, :BATCH]], axis=1)
+        lows = []
         for h in heads:
-            raw = k_ref[:, lanes_of(h)].astype(F32)
-            total = jnp.sum(raw * raw, axis=-1, keepdims=True)
-            kn = (raw * lax.rsqrt(total + 1e-06)).astype(BF16)
-            kf = kn.astype(F32)
-            kt = kf.T
-            kb = kt.astype(BF16)
-            kts[h] = kb
-            low = jnp.where(rows > cols, col_b[h] * decay_of(h) * mm(kn, kb), 0.0)
-            lows.append(low)
-            keys.append(kf)
-            turned.append(kt)
+            gram = mm(kns[h], kts[h])
+            lows.append(jnp.where(rows > cols, col_b[h] * decay_of(h) * gram, 0.0))
         inverses = []
         for c in range(0, BATCH, 2):
             inverses += list(invert_pair(lows[c], lows[c + 1], rows, cols))
@@ -209,7 +230,7 @@
             e = jnp.exp(col_g[h]) * masks[1]
             rhs = jnp.concatenate(
                 [
-                    (bt * e * keys[c]).astype(BF16),
+                    (bt * e * kns[h].astype(F32)).astype(BF16),
                     (bt * v_ref[:, lanes_of(h)].astype(F32)).astype(BF16),
                 ],
                 axis=1,
@@ -218,7 +239,7 @@
             wus[h] = wu
             rg = row_g[pl.ds(h, 1), :]
             last = col_g[h, T - 1 : T, :]
-            ends = turned[c] * (jnp.exp(last - rg) * masks[2, 0:1, :])
+            ends = kts[h].astype(F32) * (jnp.exp(last - rg) * masks[2, 0:1, :])
             both = mm(ends.astype(BF16), wu)
             diag = jnp.where(rows == cols, 1.0 - jnp.exp(last) * (keep0 * keep1), 0.0)
             ab_ref[h, 0] = (diag + both[:, :128]).astype(BF16)
@@ -228,7 +249,7 @@
     steps = HEADS // BATCH
     lax.fori_loop(0, steps, maps, 0)
     for c in range(BATCH - 1):
-        out_copy(lax.rem(me + 1 + BATCH * (steps - 1) + c, SLAB), me).start()
+        out_copy(turn(1 + BATCH * (steps - 1) + c), me).start()
     got[me] = ab_ref[me]
 
     def reads(g, _):
@@ -278,12 +299,12 @@
     total = compose(cur[3], blocks[2])
     zown[0] = (eye - total[:, :128]).astype(BF16)
     zown[1] = total[:, 128:].astype(BF16)
-    others(ZN, z, lambda i: z_copy(i, z).start())
+    later(lambda i: z_copy(i, z).start())
     entry[...] = jnp.zeros((128, 128), F32)
     lax.fori_loop(EARLY, 8, reads, 0)
-    others(ZN, z, lambda i: z_copy(i, i).wait_recv())
 
     def carry(i, _):
+        z_copy(i, i).wait_recv()
         before = entry[...]
         entry[...] = before - mm_exact(zgot[i, 0], before) + zgot[i, 1].astype(F32)
         return 0
@@ -299,14 +320,14 @@
 
     def spread(g):
         for c in range(4):
-            i = lax.rem(me + 4 * g + c, SLAB)
+            i = turn(4 * g + c)
             hi = cur[i // 8, :, :128].astype(BF16)
             value = mm(pre_a[i], jnp.concatenate([hi, hi], axis=0)) + pre_b[i]
             stage[i] = value.astype(BF16)
 
     def deliver(g, least):
         for c in range(least, 4):
-            back_copy(lax.rem(me + 4 * g + c, SLAB), me).start()
+            back_copy(turn(4 * g + c), me).start()
 
     spread(0)
     spread(1)
@@ -323,7 +344,7 @@
     loads[3].wait()
 
     def finish(g, least):
-        heads = [lax.rem(me + SLAB - (4 * g + c), SLAB) for c in range(4)]
+        heads = [turn(SLAB - (4 * g + c)) for c in range(4)]
         for i in heads[least:]:
             back_copy(i, i).wait_recv()
         for h in heads:
@@ -343,7 +364,7 @@
     lax.fori_loop(1, 8, finish_rest, 0)
     others(4, hd, lambda i: bias_copy(i, hd).wait_send())
     others(SLAB, me, lambda i: out_copy(i, me).wait_send())
-    others(ZN, z, lambda i: z_copy(i, z).wait_send())
+    later(lambda i: z_copy(i, z).wait_send())
     others(SLAB, me, lambda i: back_copy(i, me).wait_send())
 
 
@@ -351,6 +372,7 @@
     queries, key_input, value_input, gate_input,
     decay_logit, beta_logit, decay_bias, norm_gain, doc_start,
 ):
+    smem = pl.BlockSpec(memory_space=pltpu.SMEM)
     vmem = pl.BlockSpec(memory_space=pltpu.VMEM)
     hbm = pl.BlockSpec(memory_space=pl.ANY)
     dma = pltpu.SemaphoreType.DMA
@@ -359,16 +381,20 @@
     return pl.pallas_call(
         layer_kernel,
         out_shape=jax.ShapeDtypeStruct(gate_input.shape, BF16),
-        in_specs=[pl.BlockSpec(memory_space=pltpu.SMEM)] + [vmem] * 4 + [hbm] * 4,
+        in_specs=[smem] * 2 + [vmem] * 3 + [hbm] * 4,
         out_specs=vmem,
         scratch_shapes=[
             rows, rows, rows, rows,
+            pltpu.VMEM((8, T), F32),
             pltpu.VMEM((4, 8, T), F32),
+            pltpu.VMEM((HEADS, T), F32),
+            square,
             square,
             pltpu.VMEM((HEADS, T), F32),
             pltpu.VMEM((HEADS, T, T), F32),
             pltpu.VMEM((HEADS, T, T), F32),
             pltpu.VMEM((3, T, T), F32),
+            pltpu.VMEM((HEADS, T, 128), BF16),
             pltpu.VMEM((HEADS, 128, T), BF16),
             pltpu.VMEM((HEADS, T, 256), BF16),
             pltpu.VMEM((HEADS, T, 128), BF16),
@@ -390,7 +416,7 @@
         compiler_params=pltpu.CompilerParams(collective_id=0, has_side_effects=True),
     )(
         doc_start,
-        jnp.broadcast_to(decay_bias[:, None], (8, T)),
+        decay_bias,
         decay_logit.T, beta_logit.T, norm_gain[None, :],
         queries, key_input, value_input, gate_input,
     )

time: 90.7 us -> 76.8 us (0.85)
  the two profiles are of different devices: /device:TPU:1 before, /device:TPU:192 now
where the time goes in v3:
time: 76.8 us; the launch traced here: 76.7 us
  Pallas kernels  74.4 us (97%)
  local copies, waits for them, and re-layouts  2.29 us (3%)
    pallas_call x1, Pallas kernels, body(): pl.pallas_call(layer_kernel, out_shape=jax.ShapeDtypeStruct(gate_input.sh...  74.4 us
    unnamed x1, local copies, waits for them, and re-layouts  2.29 us

profile of v3, /device:TPU:192, one launch (start us, length us, event | category | flops | bytes accessed | tf_op | source)
XLA Modules:
  0.0 76.7 jit_solution(7929561421080968011)
XLA Ops:
  0.0 74.4 %shard_map.91 = bf16[128,4096]{1,0:T(8,128)(2,1)} custom-call(s32[8]{0:T(128)} %doc_ref.1, f32[8]{0:T(128)} %bias_ref.1, f32[32,128]{1,0:T(8,128)} %bitcast.3, f32[32,128]{1,0:T(8,128)} %bitcast.4, f32[1,128]{1,0:T(1,128)} %bitcast.5, bf16[128,4096]{1,0:T(8,128)(2,1)} %q_hbm.1, bf16[128,4096]{1,0:T(8,128)(2,1)} %k_hbm.1, bf16[128,4096]{1,0:T(8,128)(2,1)} %v_hbm.1, ...), custom_call_target="tpu_custom_call" | custom-call | tf_op jit(solution)/shard_map/pallas_call | solution.py:381
  74.4 2.3 %copy.11 = bf16[128,4096]{1,0:T(8,128)(2,1)} copy(bf16[128,4096]{1,0:T(8,128)(2,1)} %shard_map.91) | data formatting | bytes 2097152
